TPU v7x, 128 devices: a whole 4x4x4 slice. The times are simulated.
128 devices in a mesh: gx: 8 (over y, core), gy: 16 (over z, x).
Axes of the slice: x: 4, y: 4, z: 4, core: 2. Of those that a mesh axis runs over, the one named last changes fastest.
Arguments:
- stored: bfloat16 [128, 4096, 360], P(('gx', 'gy')), may hold values from -6 to 6
- counts: int32 [128, 128], P(('gx', 'gy')), may hold values from 0 to 32, as said below
- owners: int32 [128, 2048], P('gx', 'gy'), may hold values from 0 to 4095, as said below
- land_mask: int32 [128, 2048], P('gx', 'gy'), may hold values 0 or 1
- flow_x: float32 [128, 2048], P('gx', 'gy'), may hold values from -4 to 4
- flow_y: float32 [128, 2048], P('gx', 'gy'), may hold values from -4 to 4
- costate: float32 [3, 60, 128, 2048], P(None, None, 'gx', 'gy'), may hold values from -6 to 6
- weight_in: float32 [180, 256], replicated, may hold values from -0.4375 to 0.4375
- bias_in: float32 [256], replicated, may hold values from -3 to 3
- weight_mid: float32 [256, 256], replicated, may hold values from -0.375 to 0.375
- bias_mid: float32 [256], replicated, may hold values from -3 to 3
- weight_out: float32 [256, 60], replicated, may hold values from -0.375 to 0.375
- bias_out: float32 [60], replicated, may hold values from -4 to 4
Outputs:
- adjoint: float32 [3, 60, 128, 2048], P(None, None, 'gx', 'gy')
- grad_weight_in: float32 [180, 256], replicated
- grad_bias_in: float32 [256], replicated
- grad_weight_mid: float32 [256, 256], replicated
- grad_bias_mid: float32 [256], replicated
- grad_weight_out: float32 [256, 60], replicated
- grad_bias_out: float32 [60], replicated
Inputs may be any that keep to these rules, and one draw needn't show every extreme that they name: counts[s, d] rows of device s belong to tile d; over s they sum to 2048 for every tile; some tile takes exactly 32 rows from one device. owners[x, y] = s * 32 + r with r < counts[s, d] for the column's tile d; within a tile every value appears once.
All inputs are finite; a program needn't handle non-finite values. No bound on the sum of `land_mask` on one device may be relied on, other than what follows from the above.
Results may differ from a plain program's by a relative error of at most 0.0003.
Values may be sent and summed in bfloat16 or wider, within the bound.
No kernel may reach another device: no remote copies, remote signals or barrier semaphores. Data moves between devices by JAX's collectives and lax.ppermute only.
A program may use at most 128 MiB of HBM per device.

v0:
```python
import jax
import jax.numpy as jnp
from jax import lax
from jax.sharding import PartitionSpec as P

NZ = 60
TRACERS = 3
TSTEPS = 2
IN = 180
step_size = 0.25
flat_mix = 0.25
kappa_top = 1.5


def padded_2(value, sides, width):
    for axis, dim in sides:
        count, length = (lax.axis_size(axis), value.shape[dim])
        up = [(i, (i + 1) % count) for i in range(count - 1)]
        down = [(j, i) for i, j in up]
        last = lax.slice_in_dim(value, length - width, length, axis=dim)
        initial = lax.slice_in_dim(value, 0, width, axis=dim)
        before = lax.ppermute(last, axis, up)
        after = lax.ppermute(initial, axis, down)
        value = jnp.concatenate([before, value, after], axis=dim)
    return value


def vertical(columns, params):
    weight_in, bias_in, weight_mid, bias_mid, weight_out, bias_out = params
    hp = lax.Precision.HIGHEST
    first = jnp.tanh(jnp.dot(weight_in.T, columns, precision=hp) + bias_in[:, None])
    second = jnp.tanh(jnp.dot(weight_mid.T, first, precision=hp) + bias_mid[:, None])
    kappa = kappa_top * jax.nn.sigmoid(
        jnp.dot(weight_out.T, second, precision=hp) + bias_out[:, None]
    )
    field = columns.reshape(TRACERS, NZ, columns.shape[1])
    flux = kappa[None, :-1, :] * (field[:, 1:, :] - field[:, :-1, :])
    edge = jnp.zeros_like(flux[:, :1, :])
    upper = jnp.concatenate([flux, edge], axis=1)
    lower = jnp.concatenate([edge, flux], axis=1)
    return (upper - lower).reshape(columns.shape)


def transport(padded, padded_x, padded_y, weighted):
    near = (
        padded[..., 2:, 1:-1]
        + padded[..., :-2, 1:-1]
        + padded[..., 1:-1, 2:]
        + padded[..., 1:-1, :-2]
    )
    result = flat_mix * (near - 4.0 * weighted)
    result = result + 0.5 * (padded_x[..., 2:, 1:-1] - padded_x[..., :-2, 1:-1])
    return result + 0.5 * (padded_y[..., 1:-1, 2:] - padded_y[..., 1:-1, :-2])


def on_device(
    stored,
    counts,
    owners,
    land_mask,
    flow_x,
    flow_y,
    costate,
    weight_in,
    bias_in,
    weight_mid,
    bias_mid,
    weight_out,
    bias_out,
):
    width_x = lax.axis_size("gx")
    width_y = lax.axis_size("gy")
    devices = width_x * width_y
    tile_x, tile_y = owners.shape
    ncols = tile_x * tile_y
    slot = 2 * ncols // devices
    feat = stored.shape[2]
    my_counts = counts[0]
    starts = jnp.cumsum(my_counts) - my_counts
    row_index = jnp.minimum(
        starts[:, None] + jnp.arange(slot, dtype=jnp.int32)[None, :], stored.shape[1] - 1
    )
    outgoing = stored[0][row_index]
    arrived = lax.all_to_all(outgoing, ("gx", "gy"), split_axis=0, concat_axis=0, tiled=True)
    picked = arrived.reshape(devices * slot, feat)[owners.reshape(-1)]
    states = picked.T.reshape(TSTEPS, TRACERS, NZ, tile_x, tile_y).astype(jnp.float32)
    params = (weight_in, bias_in, weight_mid, bias_mid, weight_out, bias_out)
    totals = jax.tree.map(jnp.zeros_like, params)
    ocean = land_mask.astype(jnp.float32)
    lam = costate
    for moment in range(TSTEPS - 1, -1, -1):
        state = states[moment]
        weighted = lam * ocean
        stacked = jnp.stack([weighted, flow_x * weighted, flow_y * weighted])
        padded = padded_2(stacked, (("gx", 3), ("gy", 4)), 1)
        across = transport(padded[0], padded[1], padded[2], weighted)
        unused, pullback = jax.vjp(vertical, state.reshape(IN, ncols), params)
        grad_state, grad_params = pullback(weighted.reshape(IN, ncols))
        down = grad_state.reshape(TRACERS, NZ, tile_x, tile_y)
        lam = lam + step_size * (across + down)
        totals = jax.tree.map(lambda left, right: left + step_size * right, totals, grad_params)
    summed = lax.psum(
        (totals[0], totals[1], totals[2], totals[3], totals[4], totals[5]), ("gx", "gy")
    )
    scale = 1.0 / jnp.sqrt(jnp.float32(ncols * devices))
    return (
        lam,
        summed[0] * scale,
        summed[1] * scale,
        summed[2] * scale,
        summed[3] * scale,
        summed[4] * scale,
        summed[5] * scale,
    )


def solution(mesh):
    in_specs = (
        P(("gx", "gy"), None, None),
        P(("gx", "gy"), None),
        P("gx", "gy"),
        P("gx", "gy"),
        P("gx", "gy"),
        P("gx", "gy"),
        P(None, None, "gx", "gy"),
        P(),
        P(),
        P(),
        P(),
        P(),
        P(),
    )
    out_specs = (P(None, None, "gx", "gy"), P(), P(), P(), P(), P(), P())
    return jax.shard_map(
        on_device, mesh=mesh, in_specs=in_specs, out_specs=out_specs, check_vma=False
    )
```

profile of v0, /device:TPU:32, one launch (start us, length us, event | category | flops | bytes accessed | tf_op | source)
XLA Modules:
  0.0 549.9 jit_solution(17194821409840462331)
XLA Ops:
  21.0 17.1 %gather_fusion = bf16[4096,360]{1,0:T(8,128)(2,1)} fusion(bf16[4096,360]{1,0:T(8,128)(2,1)S(1)} %bitcast.88, s32[4096]{0:T(1024)S(1)} %broadcast_clamp_fusion), kind=kCustom, calls=%fused_computation | custom fusion | bytes 5914624 | tf_op jit(solution)/shard_map/gather | solution.py:83
  38.1 11.9 %all-to-all-start = ((bf16[128,32,360]{2,1,0:T(8,128)(2,1)}), bf16[128,32,360]{2,1,0:T(8,128)(2,1)S(1)}, u32[]{:S(2)}, u32[]{:S(2)}) async-start(bf16[128,32,360]{2,1,0:T(8,128)(2,1)} %bitcast.94), calls=%async_computation | async-start | bytes 6291456 | tf_op jit(solution)/shard_map/all_to_all | solution.py:84
  50.1 5.1 pad_maximum_fusion.2
  55.2 11.3 %fusion.61 = (f32[3,3,60,18,1]{4,3,2,1,0:T(8,128)}, f32[3,3,60,18,1]{4,3,2,1,0:T(8,128)}) fusion(f32[3,3,60,18,128]{4,3,2,1,0:T(8,128)} %pad_maximum_fusion.2), kind=kLoop, calls=%fused_computation.134 | loop fusion | bytes 155520 | tf_op jit(solution)/shard_map/slice | solution.py:20
  66.6 4.5 copy.64
  74.5 5.2 copy.65
  79.7 4.8 collective-permute-start.3
  89.1 5.2 copy.66
  94.3 5.3 copy.67
  99.6 16.7 %pad_maximum_fusion = f32[3,3,60,18,130]{4,3,2,1,0:T(8,128)} fusion(f32[3,3,60,18,1]{4,3,2,1,0:T(8,128)} %copy.67, f32[3,3,60,1,128]{4,3,2,1,0:T(1,128)} %collective-permute-done.1, f32[1,3,60,16,128]{4,3,2,1,0:T(8,128)} %copy-done.14, f32[1,3,60,16,128]{4,3,2,1,0:T(8,128)} %copy-done.13, f32[1,3,60,16,128]{4,3,2,1,0:T(8,128)} %copy-done.12, ...), kind=kLoop, calls=%fused_computation.2 | loop fusion | flops 7581600 | bytes 10108800 | tf_op jit(solution)/shard_map/concatenate | solution.py:24
  116.2 9.9 %slice_bitcast_fusion.5 = (f32[3,60,18,130]{3,2,1,0:T(8,128)}, f32[3,60,18,130]{3,2,1,0:T(8,128)}, f32[3,60,18,130]{3,2,1,0:T(8,128)}) fusion(f32[3,3,60,18,130]{4,3,2,1,0:T(8,128)} %pad_maximum_fusion), kind=kLoop, calls=%fused_computation.11 | loop fusion | bytes 10108800 | tf_op jit(solution)/shard_map/squeeze | solution.py:96
  126.1 9.3 %gather_fusion.1 = bf16[2048,360]{1,0:T(8,128)(2,1)} fusion(bf16[4096,360]{1,0:T(8,128)(2,1)S(1)} %bitcast.89, s32[2048]{0:T(1024)S(1)} %broadcast_clamp_fusion.1), kind=kCustom, calls=%fused_computation.1 | custom fusion | bytes 2957312 | tf_op jit(solution)/shard_map/gather | solution.py:85
  162.7 3.9 fusion.63
  168.2 4.5 fusion.4
  174.3 11.8 %fusion.49 = (f32[1,3,60,16,128]{4,3,2,1,0:T(8,128)}, f32[3,60,16,128]{3,2,1,0:T(8,128)S(1)}) fusion(f32[16,128]{1,0:T(8,128)S(1)} %convert_element_type.7, f32[3,60,16,128]{3,2,1,0:T(8,128)S(1)} %copy-done.30, f32[3,60,16,128]{3,2,1,0:T(8,128)S(1)} %bitcast.100, f32[3,60,18,130]{3,2,1,0:T(8,128)} %get-tuple-element.37, ...), kind=kLoop, calls=%fused_computation.106 | loop fusion | flops 6266880 | bytes 17702912 | tf_op jit(solution)/shard_map/stack | solution.py:94
  205.3 5.9 %fusion.58 = (f32[3,59,2048]{2,1,0:T(8,128)}, f32[3,59,2048]{2,1,0:T(8,128)}, f32[59,2048]{1,0:T(8,128)S(1)}) fusion(f32[3,60,2048]{2,1,0:T(8,128)} %reshape_reshape.7, f32[59,2048]{1,0:T(8,128)} %slice_multiply_fusion, f32[3,60,2048]{2,1,0:T(8,128)} %reshape_reshape_squeeze.7), kind=kLoop, calls=%fused_computation.131 | loop fusion | flops 2416640 | bytes 9666560 | tf_op jit(solution)/shard_map/transpose(jvp())/neg | solution.py:37
  213.6 4.3 fusion.67
  225.3 65.3 %all-reduce.6 = (f32[256]{0:T(256)S(1)}, f32[256]{0:T(256)S(1)}, f32[256,60]{0,1:T(8,128)S(1)}, f32[60]{0:T(128)S(1)}) all-reduce(f32[256]{0:T(256)S(1)} %add_multiply_fusion.1, f32[256]{0:T(256)S(1)} %add_multiply_fusion, f32[256,60]{0,1:T(8,128)S(1)} %fusion.40, ...), channel_id=1, replica_groups=mesh['gx'=8,'gy'=16] {'gx','gy'}, use_global_device_ids=true, to_apply=%region_6.7 | all-reduce | flops 15932 | bytes 127456 | tf_op jit(solution)/shard_map/psum | solution.py:102
  291.2 6.5 %fusion.38 = f32[256,256]{1,0:T(8,128)} fusion(f32[256,256]{1,0:T(8,128)} %fusion.67, f32[2048,256]{1,0:T(8,128)} %fusion.2, f32[2048,256]{1,0:T(8,128)} %copy-done.19), kind=kOutput, calls=%fused_computation.85 | convolution fusion | flops 1610743808 | bytes 4718592 | tf_op jit(solution)/shard_map/transpose(jvp())/dot_general | solution.py:32
  306.6 3.7 fusion.39
  310.3 4.3 fusion.5
  317.3 140.6 %all-reduce.10.cloned.1.call-done = (f32[180,256]{1,0:T(8,128)}, f32[256,256]{1,0:T(8,128)}) async-done(((f32[180,256]{1,0:T(8,128)}, f32[256,256]{1,0:T(8,128)}), (f32[180,256]{1,0:T(8,128)}, f32[256,256]{1,0:T(8,128)})) %all-reduce.10.cloned.1.call-update) | async-done | bytes 446480 | tf_op jit(solution)/shard_map/psum | solution.py:102
  459.6 4.9 pad_maximum_fusion.3
  464.5 11.3 %fusion.60 = (f32[3,3,60,18,1]{4,3,2,1,0:T(8,128)}, f32[3,3,60,18,1]{4,3,2,1,0:T(8,128)}) fusion(f32[3,3,60,18,128]{4,3,2,1,0:T(8,128)} %pad_maximum_fusion.3), kind=kLoop, calls=%fused_computation.133 | loop fusion | bytes 155520 | tf_op jit(solution)/shard_map/slice | solution.py:20
  475.8 4.5 copy.71
  483.5 5.2 copy.72
  488.8 4.8 collective-permute-start.7
  494.3 5.2 copy.73
  499.4 5.3 copy.74
  504.7 16.2 %pad_maximum_fusion.1 = f32[3,3,60,18,130]{4,3,2,1,0:T(8,128)} fusion(f32[3,3,60,18,1]{4,3,2,1,0:T(8,128)} %copy.74, f32[3,3,60,1,128]{4,3,2,1,0:T(1,128)} %collective-permute-done.5, f32[1,3,60,16,128]{4,3,2,1,0:T(8,128)S(1)} %copy-done.11, f32[1,3,60,16,128]{4,3,2,1,0:T(8,128)S(1)} %get-tuple-element.51, f32[1,3,60,16,128]{4,3,2,1,0:T(8,128)} %get-tuple-element.27, ...), kind=kLoop, calls=%fused_computation.3 | loop fusion | flops 7581600 | bytes 10108800 | tf_op jit(solution)/shard_map/concatenate | solution.py:24
  520.8 10.1 %slice_bitcast_fusion.2 = (f32[3,60,18,130]{3,2,1,0:T(8,128)}, f32[3,60,18,130]{3,2,1,0:T(8,128)}, f32[3,60,18,130]{3,2,1,0:T(8,128)}) fusion(f32[3,3,60,18,130]{4,3,2,1,0:T(8,128)} %pad_maximum_fusion.1), kind=kLoop, calls=%fused_computation.8 | loop fusion | bytes 10108800 | tf_op jit(solution)/shard_map/squeeze | solution.py:96
  530.9 11.7 %fusion.24 = f32[3,60,16,128]{3,2,1,0:T(8,128)} fusion(f32[3,60,16,128]{3,2,1,0:T(8,128)S(1)} %copy-done.22, f32[3,60,16,128]{3,2,1,0:T(8,128)S(1)} %bitcast.99, f32[3,60,18,130]{3,2,1,0:T(8,128)} %get-tuple-element.34, f32[3,60,18,130]{3,2,1,0:T(8,128)} %get-tuple-element.35, f32[3,60,18,130]{3,2,1,0:T(8,128)} %get-tuple-element.33, ...), kind=kLoop, calls=%fused_computation.57 | loop fusion | flops 5898240 | bytes 16228352 | tf_op jit(solution)/shard_map/add | solution.py:100
  (163 shorter events, 98.8 us)
Async XLA Ops:
  7.2 133.6 %copy-start = (f32[256,256]{1,0:T(8,128)S(1)}, f32[256,256]{1,0:T(8,128)}, u32[]{:S(2)}) copy-start(f32[256,256]{1,0:T(8,128)} %param.22) | copy-start | bytes 786436
  13.1 37.0 %collective-permute-start = (f32[3,3,60,1,128]{4,3,2,1,0:T(1,128)}, f32[3,3,60,1,128]{4,3,2,1,0:T(1,128)}, u32[]{:S(2)}, u32[]{:S(2)}) collective-permute-start(f32[3,3,60,1,128]{4,3,2,1,0:T(1,128)} %get-tuple-element.45), channel_id=1, source_target_pairs={{0,16},{16,32},{32,48},{48,64},{64,80},{80,96},{96,112},{1,17},{17... | collective-permute-start | bytes 829448 | tf_op jit(solution)/shard_map/ppermute | solution.py:22
  15.5 4.8 copy-start.43
  15.5 34.6 %collective-permute-start.1 = (f32[3,3,60,1,128]{4,3,2,1,0:T(1,128)}, f32[3,3,60,1,128]{4,3,2,1,0:T(1,128)}, u32[]{:S(2)}, u32[]{:S(2)}) collective-permute-start(f32[3,3,60,1,128]{4,3,2,1,0:T(1,128)} %get-tuple-element.46), channel_id=1, source_target_pairs={{16,0},{32,16},{48,32},{64,48},{80,64},{96,80},{112,96},{17,1},{33... | collective-permute-start | bytes 829448 | tf_op jit(solution)/shard_map/ppermute | solution.py:23
  38.1 12.0 %copy-start.37 = (s32[16,128]{1,0:T(8,128)S(1)}, s32[16,128]{1,0:T(8,128)}, u32[]{:S(2)}) copy-start(s32[16,128]{1,0:T(8,128)} %param.15) | copy-start | bytes 24580
  38.1 88.0 %all-to-all-start = ((bf16[128,32,360]{2,1,0:T(8,128)(2,1)}), bf16[128,32,360]{2,1,0:T(8,128)(2,1)S(1)}, u32[]{:S(2)}, u32[]{:S(2)}) async-start(bf16[128,32,360]{2,1,0:T(8,128)(2,1)} %bitcast.94), calls=%async_computation | async-start | bytes 6291456 | tf_op jit(solution)/shard_map/all_to_all | solution.py:84
  50.0 407.9 %all-reduce.10.cloned.1.call-start = ((), (), s32[]{:S(2)}) async-start(), calls=%async_computation.1 | async-start | bytes 901120 | tf_op jit(solution)/shard_map/psum | solution.py:102
  71.1 18.0 %collective-permute-start.2 = (f32[3,3,60,18,1]{2,4,3,1,0:T(1,128)S(1)}, f32[3,3,60,18,1]{2,4,3,1,0:T(1,128)}, u32[]{:S(2)}, u32[]{:S(2)}) collective-permute-start(f32[3,3,60,18,1]{2,4,3,1,0:T(1,128)S(1)} %copy.64), channel_id=1, source_target_pairs={{0,1},{1,2},{2,3},{3,4},{4,5},{5,6},{6,7},{7,8},{8,9},{9,10},{10,1... | collective-permute-start | bytes 116648 | tf_op jit(solution)/shard_map/ppermute | solution.py:22
  79.7 14.6 %collective-permute-start.3 = (f32[3,3,60,18,1]{2,4,3,1,0:T(1,128)}, f32[3,3,60,18,1]{2,4,3,1,0:T(1,128)}, u32[]{:S(2)}, u32[]{:S(2)}) collective-permute-start(f32[3,3,60,18,1]{2,4,3,1,0:T(1,128)} %copy.65), channel_id=1, source_target_pairs={{1,0},{2,1},{3,2},{4,3},{5,4},{6,5},{7,6},{8,7},{9,8},{10,9},{11,1... | collective-permute-start | bytes 116648 | tf_op jit(solution)/shard_map/ppermute | solution.py:23
  138.4 4.3 copy-start.3
  174.3 11.8 %copy-start.35 = (f32[16,128]{1,0:T(8,128)S(1)}, f32[16,128]{1,0:T(8,128)}, u32[]{:S(2)}) copy-start(f32[16,128]{1,0:T(8,128)} %param.17) | copy-start | bytes 24580
  174.3 11.8 %copy-start.36 = (f32[16,128]{1,0:T(8,128)S(1)}, f32[16,128]{1,0:T(8,128)}, u32[]{:S(2)}) copy-start(f32[16,128]{1,0:T(8,128)} %param.18) | copy-start | bytes 24580
  190.9 4.9 copy-start.42
  205.3 5.9 %copy-start.24 = (f32[60,2048]{1,0:T(8,128)S(1)}, f32[60,2048]{1,0:T(8,128)}, u32[]{:S(2)}) copy-start(f32[60,2048]{1,0:T(8,128)} %copy-done.23) | copy-start | bytes 1474564
  205.3 6.1 %copy-start.7 = (f32[2048,256]{1,0:T(8,128)S(1)}, f32[2048,256]{1,0:T(8,128)}, u32[]{:S(2)}) copy-start(f32[2048,256]{1,0:T(8,128)} %copy-done.6) | copy-start | bytes 6291460
  213.6 8.1 %copy-start.19 = (f32[2048,256]{1,0:T(8,128)}, f32[2048,256]{1,0:T(8,128)S(1)}, u32[]{:S(2)}) copy-start(f32[2048,256]{1,0:T(8,128)S(1)} %get-tuple-element.65) | copy-start | bytes 6291460
  213.6 4.3 copy-start.18
  221.9 3.3 copy-start.44
  221.9 3.3 copy-start.40
  291.2 6.5 %copy-start.10 = (f32[1,3,60,16,128]{4,3,2,1,0:T(8,128)S(1)}, f32[1,3,60,16,128]{4,3,2,1,0:T(8,128)}, u32[]{:S(2)}) copy-start(f32[1,3,60,16,128]{4,3,2,1,0:T(8,128)} %get-tuple-element.52) | copy-start | bytes 4423684
  291.2 6.5 %copy-start.15 = (f32[1,3,60,16,128]{4,3,2,1,0:T(8,128)S(1)}, f32[1,3,60,16,128]{4,3,2,1,0:T(8,128)}, u32[]{:S(2)}) copy-start(f32[1,3,60,16,128]{4,3,2,1,0:T(8,128)} %get-tuple-element.27) | copy-start | bytes 4423684
  297.7 4.8 copy-start.27
  297.7 4.8 copy-start.28
  298.9 160.6 %collective-permute-start.4 = (f32[3,3,60,1,128]{4,3,2,1,0:T(1,128)}, f32[3,3,60,1,128]{4,3,2,1,0:T(1,128)}, u32[]{:S(2)}, u32[]{:S(2)}) collective-permute-start(f32[3,3,60,1,128]{4,3,2,1,0:T(1,128)} %get-tuple-element.43), channel_id=1, source_target_pairs={{0,16},{16,32},{32,48},{48,64},{64,80},{80,96},{96,112},{1,17},{17... | collective-permute-start | bytes 829448 | tf_op jit(solution)/shard_map/ppermute | solution.py:22
  301.2 158.3 %collective-permute-start.5 = (f32[3,3,60,1,128]{4,3,2,1,0:T(1,128)}, f32[3,3,60,1,128]{4,3,2,1,0:T(1,128)}, u32[]{:S(2)}, u32[]{:S(2)}) collective-permute-start(f32[3,3,60,1,128]{4,3,2,1,0:T(1,128)} %get-tuple-element.44), channel_id=1, source_target_pairs={{16,0},{32,16},{48,32},{64,48},{80,64},{96,80},{112,96},{17,1},{33... | collective-permute-start | bytes 829448 | tf_op jit(solution)/shard_map/ppermute | solution.py:23
  306.6 3.7 copy-start.32
  316.0 143.6 %copy-start.11 = (f32[1,3,60,16,128]{4,3,2,1,0:T(8,128)S(1)}, f32[1,3,60,16,128]{4,3,2,1,0:T(8,128)}, u32[]{:S(2)}) copy-start(f32[1,3,60,16,128]{4,3,2,1,0:T(8,128)} %get-tuple-element.52) | copy-start | bytes 4423684
  480.4 13.9 %collective-permute-start.6 = (f32[3,3,60,18,1]{2,4,3,1,0:T(1,128)S(1)}, f32[3,3,60,18,1]{2,4,3,1,0:T(1,128)}, u32[]{:S(2)}, u32[]{:S(2)}) collective-permute-start(f32[3,3,60,18,1]{2,4,3,1,0:T(1,128)S(1)} %copy.71), channel_id=1, source_target_pairs={{0,1},{1,2},{2,3},{3,4},{4,5},{5,6},{6,7},{7,8},{8,9},{9,10},{10,1... | collective-permute-start | bytes 116648 | tf_op jit(solution)/shard_map/ppermute | solution.py:22
  483.5 10.0 %copy-start.34 = (f32[180,256]{1,0:T(8,128)S(1)}, f32[180,256]{1,0:T(8,128)}, u32[]{:S(2)}) copy-start(f32[180,256]{1,0:T(8,128)} %get-tuple-element.25) | copy-start | bytes 552964
  488.8 10.7 %collective-permute-start.7 = (f32[3,3,60,18,1]{2,4,3,1,0:T(1,128)}, f32[3,3,60,18,1]{2,4,3,1,0:T(1,128)}, u32[]{:S(2)}, u32[]{:S(2)}) collective-permute-start(f32[3,3,60,18,1]{2,4,3,1,0:T(1,128)} %copy.72), channel_id=1, source_target_pairs={{1,0},{2,1},{3,2},{4,3},{5,4},{6,5},{7,6},{8,7},{9,8},{10,9},{11,1... | collective-permute-start | bytes 116648 | tf_op jit(solution)/shard_map/ppermute | solution.py:23
  520.8 10.1 %copy-start.22 = (f32[3,60,16,128]{3,2,1,0:T(8,128)S(1)}, f32[3,60,16,128]{3,2,1,0:T(8,128)}, u32[]{:S(2)}) copy-start(f32[3,60,16,128]{3,2,1,0:T(8,128)} %copy-done.21) | copy-start | bytes 4423684
  520.8 10.1 %copy-start.29 = (f32[180,16,128]{2,1,0:T(8,128)S(1)}, f32[180,16,128]{2,1,0:T(8,128)}, u32[]{:S(2)}) copy-start(f32[180,16,128]{2,1,0:T(8,128)} %slice.203) | copy-start | bytes 4423684
  (23 other events, 45.2 us)
Sparse Core Ops, SparseCore 0:
  315.3 142.5 all-reduce.9
where the time goes:
time: 556 us; the launch traced here: 550 us
  local copies, waits for them, and re-layouts  144 us (26%)
  waiting for transfers between devices  143 us (26%)
  other arithmetic  94 us (17%)
  blocking collectives  65.3 us (12%)
  matrix products  53.1 us (10%)
  starting transfers between devices  35.5 us (6%)
  between operations  15.1 us (3%)
    psum x1, waiting for transfers between devices, on_device(): lax.psum((totals[0], totals[1], totals[2], totals[3], totals[4], totals[5...  141 us
    psum x1, blocking collectives, on_device(): lax.psum((totals[0], totals[1], totals[2], totals[3], totals[4], totals[5...  65.3 us
    concatenate x4, other arithmetic, padded_2(): value = jnp.concatenate([before, value, after], axis=dim)  42.8 us
    slice x4, local copies, waits for them, and re-layouts, padded_2(): last = lax.slice_in_dim(value, length - width, length, axis=dim)  31.7 us
    dot_general x6, matrix products, vertical(): jnp.dot(weight_mid.T, first, precision=hp) + bias_mid[:, None]  23.4 us
    squeeze x2, local copies, waits for them, and re-layouts, on_device(): across = transport(padded[0], padded[1], padded[2], weighted)  20 us
    dot_general x6, matrix products, vertical(): jnp.dot(weight_in.T, columns, precision=hp) + bias_in[:, None]  18.3 us
    gather x1, local copies, waits for them, and re-layouts, on_device(): outgoing = stored[0][row_index]  17.1 us
  transfers between devices with their start and end apart: 10, of which 2 were waited for; matrix products, arithmetic and copies ran while one was open for 21% of the time, Pallas kernels for 0%

commit v1 on v0

--- a/solution.py
+++ b/solution.py
@@ -100,7 +100,7 @@
         lam = lam + step_size * (across + down)
         totals = jax.tree.map(lambda left, right: left + step_size * right, totals, grad_params)
     summed = lax.psum(
-        (totals[0], totals[1], totals[2], totals[3], totals[4], totals[5]), ("gx", "gy")
+        lax.psum((totals[0], totals[1], totals[2], totals[3], totals[4], totals[5]), "gx"), "gy"
     )
     scale = 1.0 / jnp.sqrt(jnp.float32(ncols * devices))
     return (

time: 556 us -> 516 us (0.928)
  waiting for transfers between devices: 143 us -> 67.6 us
  blocking collectives: 65.3 us -> 93.9 us
    psum x1, waiting for transfers between devices: 141 us -> 26.3 us  [on_device(): lax.psum((totals[0], totals[1], totals[2], totals[3], totals[4], totals[5...]
    psum x0 -> x1, blocking collectives: none -> 68 us  [on_device(): lax.psum(lax.psum((totals[0], totals[1], totals[2], totals[3], totals[4],...]
    psum x1, blocking collectives: 65.3 us -> 25.9 us  [on_device(): lax.psum((totals[0], totals[1], totals[2], totals[3], totals[4], totals[5...]
    psum x0 -> x1, waiting for transfers between devices: none -> 39.3 us  [on_device(): lax.psum(lax.psum((totals[0], totals[1], totals[2], totals[3], totals[4],...]
    unnamed x95 -> x99, local copies, waits for them, and re-layouts: 11.2 us -> 15 us
  transfers between devices with their start and end apart: 10 -> 11, of which waited for: 2 -> 3; matrix products, arithmetic and copies ran while one was open for 21% -> 35% of each run, Pallas kernels for 0% -> 0%
where the time goes in v1:
time: 516 us; the launch traced here: 508 us
  local copies, waits for them, and re-layouts  147 us (28%)
  other arithmetic  94.8 us (18%)
  blocking collectives  93.9 us (18%)
  waiting for transfers between devices  67.6 us (13%)
  matrix products  54.3 us (11%)
  starting transfers between devices  35.2 us (7%)
  between operations  15.1 us (3%)
    psum x1, blocking collectives, on_device(): lax.psum(lax.psum((totals[0], totals[1], totals[2], totals[3], totals[4],...  68 us
    concatenate x4, other arithmetic, padded_2(): value = jnp.concatenate([before, value, after], axis=dim)  42.6 us
    psum x1, waiting for transfers between devices, on_device(): lax.psum(lax.psum((totals[0], totals[1], totals[2], totals[3], totals[4],...  39.3 us
    slice x4, local copies, waits for them, and re-layouts, padded_2(): last = lax.slice_in_dim(value, length - width, length, axis=dim)  31.7 us
    psum x1, waiting for transfers between devices, on_device(): lax.psum((totals[0], totals[1], totals[2], totals[3], totals[4], totals[5...  26.3 us
    psum x1, blocking collectives, on_device(): lax.psum((totals[0], totals[1], totals[2], totals[3], totals[4], totals[5...  25.9 us
    dot_general x6, matrix products, vertical(): jnp.dot(weight_mid.T, first, precision=hp) + bias_mid[:, None]  23.4 us
    squeeze x2, local copies, waits for them, and re-layouts, on_device(): across = transport(padded[0], padded[1], padded[2], weighted)  20 us
  transfers between devices with their start and end apart: 11, of which 3 were waited for; matrix products, arithmetic and copies ran while one was open for 35% of the time, Pallas kernels for 0%

profile of v1, /device:TPU:32, one launch (start us, length us, event | category | flops | bytes accessed | tf_op | source)
XLA Modules:
  0.0 508.2 jit_solution(7650229565232812615)
XLA Ops:
  21.0 17.1 %gather_fusion = bf16[4096,360]{1,0:T(8,128)(2,1)} fusion(bf16[4096,360]{1,0:T(8,128)(2,1)S(1)} %bitcast.88, s32[4096]{0:T(1024)S(1)} %broadcast_clamp_fusion), kind=kCustom, calls=%fused_computation | custom fusion | bytes 5914624 | tf_op jit(solution)/shard_map/gather | solution.py:83
  38.1 11.9 %all-to-all-start = ((bf16[128,32,360]{2,1,0:T(8,128)(2,1)}), bf16[128,32,360]{2,1,0:T(8,128)(2,1)S(1)}, u32[]{:S(2)}, u32[]{:S(2)}) async-start(bf16[128,32,360]{2,1,0:T(8,128)(2,1)} %bitcast.94), calls=%async_computation | async-start | bytes 6291456 | tf_op jit(solution)/shard_map/all_to_all | solution.py:84
  50.2 5.1 pad_maximum_fusion.2
  55.2 11.3 %fusion.61 = (f32[3,3,60,18,1]{4,3,2,1,0:T(8,128)}, f32[3,3,60,18,1]{4,3,2,1,0:T(8,128)}) fusion(f32[3,3,60,18,128]{4,3,2,1,0:T(8,128)} %pad_maximum_fusion.2), kind=kLoop, calls=%fused_computation.134 | loop fusion | bytes 155520 | tf_op jit(solution)/shard_map/slice | solution.py:20
  66.6 4.5 copy.64
  74.5 5.2 %copy.65 = f32[3,3,60,18,1]{2,4,3,1,0:T(1,128)} copy(f32[3,3,60,18,1]{4,3,2,1,0:T(8,128)} %get-tuple-element.48) | data formatting | bytes 77760 | tf_op jit(solution)/shard_map/slice | solution.py:21
  79.7 4.8 collective-permute-start.3
  89.2 5.2 %copy.66 = f32[3,3,60,18,1]{4,3,2,1,0:T(8,128)} copy(f32[3,3,60,18,1]{2,4,3,1,0:T(1,128)} %collective-permute-done.2) | data formatting | bytes 77760 | tf_op jit(solution)/shard_map/ppermute | solution.py:22
  94.3 5.2 %copy.67 = f32[3,3,60,18,1]{4,3,2,1,0:T(8,128)} copy(f32[3,3,60,18,1]{2,4,3,1,0:T(1,128)} %collective-permute-done.3) | data formatting | bytes 77760 | tf_op jit(solution)/shard_map/ppermute | solution.py:23
  99.6 16.7 %pad_maximum_fusion = f32[3,3,60,18,130]{4,3,2,1,0:T(8,128)} fusion(f32[3,3,60,18,1]{4,3,2,1,0:T(8,128)} %copy.67, f32[3,3,60,1,128]{4,3,2,1,0:T(1,128)} %collective-permute-done.1, f32[1,3,60,16,128]{4,3,2,1,0:T(8,128)} %copy-done.14, f32[1,3,60,16,128]{4,3,2,1,0:T(8,128)} %copy-done.13, f32[1,3,60,16,128]{4,3,2,1,0:T(8,128)} %copy-done.12, ...), kind=kLoop, calls=%fused_computation.2 | loop fusion | flops 7581600 | bytes 10108800 | tf_op jit(solution)/shard_map/concatenate | solution.py:24
  116.2 9.9 %slice_bitcast_fusion.5 = (f32[3,60,18,130]{3,2,1,0:T(8,128)}, f32[3,60,18,130]{3,2,1,0:T(8,128)}, f32[3,60,18,130]{3,2,1,0:T(8,128)}) fusion(f32[3,3,60,18,130]{4,3,2,1,0:T(8,128)} %pad_maximum_fusion), kind=kLoop, calls=%fused_computation.11 | loop fusion | bytes 10108800 | tf_op jit(solution)/shard_map/squeeze | solution.py:96
  126.1 9.3 %gather_fusion.1 = bf16[2048,360]{1,0:T(8,128)(2,1)} fusion(bf16[4096,360]{1,0:T(8,128)(2,1)S(1)} %bitcast.89, s32[2048]{0:T(1024)S(1)} %broadcast_clamp_fusion.1), kind=kCustom, calls=%fused_computation.1 | custom fusion | bytes 2957312 | tf_op jit(solution)/shard_map/gather | solution.py:85
  168.2 4.5 fusion.4
  174.4 11.8 %fusion.49 = (f32[1,3,60,16,128]{4,3,2,1,0:T(8,128)}, f32[3,60,16,128]{3,2,1,0:T(8,128)S(1)}) fusion(f32[16,128]{1,0:T(8,128)S(1)} %convert_element_type.7, f32[3,60,16,128]{3,2,1,0:T(8,128)S(1)} %copy-done.33, f32[3,60,16,128]{3,2,1,0:T(8,128)S(1)} %bitcast.100, f32[3,60,18,130]{3,2,1,0:T(8,128)} %get-tuple-element.43, ...), kind=kLoop, calls=%fused_computation.106 | loop fusion | flops 6266880 | bytes 17702912 | tf_op jit(solution)/shard_map/stack | solution.py:94
  205.4 6.0 %fusion.58 = (f32[3,59,2048]{2,1,0:T(8,128)}, f32[3,59,2048]{2,1,0:T(8,128)}, f32[59,2048]{1,0:T(8,128)S(1)}) fusion(f32[3,60,2048]{2,1,0:T(8,128)} %reshape_reshape.7, f32[59,2048]{1,0:T(8,128)} %slice_multiply_fusion, f32[3,60,2048]{2,1,0:T(8,128)} %reshape_reshape_squeeze.7), kind=kLoop, calls=%fused_computation.131 | loop fusion | flops 2416640 | bytes 9666560 | tf_op jit(solution)/shard_map/transpose(jvp())/neg | solution.py:37
  215.9 4.3 fusion.67
  227.5 25.9 %all-reduce.8 = (f32[256]{0:T(256)S(1)}, f32[256]{0:T(256)S(1)}, f32[256,60]{0,1:T(8,128)S(1)}, f32[60]{0:T(128)S(1)}) all-reduce(f32[256]{0:T(256)S(1)} %get-tuple-element.73, f32[256]{0:T(256)S(1)} %get-tuple-element.72, f32[256,60]{0,1:T(8,128)S(1)} %fusion.40, f32[60]{0:T(128)S(1)} %add_multiply_fusion.2), channel_id=1, replica_groups=mesh['gx'=8,'gy'=16] {'gx'}, use_global_device_ids=true, to_apply=%region_7.8 | all-reduce | flops 15932 | bytes 127456 | tf_op jit(solution)/shard_map/psum | solution.py:103
  253.4 68.0 %all-reduce.6 = (f32[256]{0:T(256)S(1)}, f32[256]{0:T(256)S(1)}, f32[256,60]{0,1:T(8,128)}, f32[60]{0:T(128)S(1)}) all-reduce(f32[256]{0:T(256)S(1)} %get-tuple-element.27, f32[256]{0:T(256)S(1)} %get-tuple-element.28, f32[256,60]{0,1:T(8,128)S(1)} %get-tuple-element.29, ...), channel_id=1, replica_groups=mesh['gx'=8,'gy'=16] {'gy'}, use_global_device_ids=true, to_apply=%region_8.9 | all-reduce | flops 15932 | bytes 127456 | tf_op jit(solution)/shard_map/psum | solution.py:102
  321.9 6.5 %fusion.38 = f32[256,256]{1,0:T(8,128)} fusion(f32[256,256]{1,0:T(8,128)} %fusion.67, f32[2048,256]{1,0:T(8,128)} %fusion.2, f32[2048,256]{1,0:T(8,128)} %copy-done.19), kind=kOutput, calls=%fused_computation.85 | convolution fusion | flops 1610743808 | bytes 4718592 | tf_op jit(solution)/shard_map/transpose(jvp())/dot_general | solution.py:32
  340.7 5.6 %fusion.5 = f32[180,2048]{1,0:T(8,128)} fusion(f32[180,2048]{1,0:T(8,128)} %reshape.182, f32[2048,256]{1,0:T(8,128)} %get-tuple-element.67, f32[180,256]{1,0:T(8,128)S(1)} %copy-done.35), kind=kOutput, calls=%fused_computation.27 | convolution fusion | flops 1132830720 | bytes 5230592 | tf_op jit(solution)/shard_map/transpose(jvp())/dot_general | solution.py:31
  347.6 4.6 pad_maximum_fusion.3
  352.2 11.3 %fusion.60 = (f32[3,3,60,18,1]{4,3,2,1,0:T(8,128)}, f32[3,3,60,18,1]{4,3,2,1,0:T(8,128)}) fusion(f32[3,3,60,18,128]{4,3,2,1,0:T(8,128)} %pad_maximum_fusion.3), kind=kLoop, calls=%fused_computation.133 | loop fusion | bytes 155520 | tf_op jit(solution)/shard_map/slice | solution.py:20
  363.5 4.5 copy.71
  370.0 4.8 copy.72
  374.8 6.0 %collective-permute-start.7 = (f32[3,3,60,18,1]{2,4,3,1,0:T(1,128)S(1)}, f32[3,3,60,18,1]{2,4,3,1,0:T(1,128)}, u32[]{:S(2)}, u32[]{:S(2)}) collective-permute-start(f32[3,3,60,18,1]{2,4,3,1,0:T(1,128)S(1)} %copy.72), channel_id=1, source_target_pairs={{1,0},{2,1},{3,2},{4,3},{5,4},{6,5},{7,6},{8,7},{9,8},{10,9},{11,1... | collective-permute-start | bytes 116648 | tf_op jit(solution)/shard_map/ppermute | solution.py:23
  384.3 26.3 %all-reduce.15.cloned.1.call-done = (f32[180,256]{1,0:T(8,128)}, f32[256,256]{1,0:T(8,128)}) async-done(((f32[180,256]{1,0:T(8,128)}, f32[256,256]{1,0:T(8,128)}), (f32[180,256]{1,0:T(8,128)}, f32[256,256]{1,0:T(8,128)})) %all-reduce.15.cloned.1.call-update) | async-done | bytes 446480 | tf_op jit(solution)/shard_map/psum | solution.py:103
  410.6 4.5 copy.73
  415.1 5.2 %copy.74 = f32[3,3,60,18,1]{4,3,2,1,0:T(8,128)} copy(f32[3,3,60,18,1]{2,4,3,1,0:T(1,128)} %collective-permute-done.7) | data formatting | bytes 77760 | tf_op jit(solution)/shard_map/ppermute | solution.py:23
  420.3 16.3 %pad_maximum_fusion.1 = f32[3,3,60,18,130]{4,3,2,1,0:T(8,128)} fusion(f32[3,3,60,18,1]{4,3,2,1,0:T(8,128)} %copy.74, f32[3,3,60,1,128]{4,3,2,1,0:T(1,128)} %collective-permute-done.5, f32[1,3,60,16,128]{4,3,2,1,0:T(8,128)S(1)} %copy-done.11, f32[1,3,60,16,128]{4,3,2,1,0:T(8,128)S(1)} %get-tuple-element.57, f32[1,3,60,16,128]{4,3,2,1,0:T(8,128)} %get-tuple-element.33, ...), kind=kLoop, calls=%fused_computation.3 | loop fusion | flops 7581600 | bytes 10108800 | tf_op jit(solution)/shard_map/concatenate | solution.py:24
  436.6 10.1 %slice_bitcast_fusion.2 = (f32[3,60,18,130]{3,2,1,0:T(8,128)}, f32[3,60,18,130]{3,2,1,0:T(8,128)}, f32[3,60,18,130]{3,2,1,0:T(8,128)}) fusion(f32[3,3,60,18,130]{4,3,2,1,0:T(8,128)} %pad_maximum_fusion.1), kind=kLoop, calls=%fused_computation.8 | loop fusion | bytes 10108800 | tf_op jit(solution)/shard_map/squeeze | solution.py:96
  446.6 11.7 %fusion.24 = f32[3,60,16,128]{3,2,1,0:T(8,128)} fusion(f32[3,60,16,128]{3,2,1,0:T(8,128)S(1)} %copy-done.22, f32[3,60,16,128]{3,2,1,0:T(8,128)S(1)} %bitcast.99, f32[3,60,18,130]{3,2,1,0:T(8,128)} %get-tuple-element.40, f32[3,60,18,130]{3,2,1,0:T(8,128)} %get-tuple-element.41, f32[3,60,18,130]{3,2,1,0:T(8,128)} %get-tuple-element.39, ...), kind=kLoop, calls=%fused_computation.57 | loop fusion | flops 5898240 | bytes 16228352 | tf_op jit(solution)/shard_map/add | solution.py:100
  458.3 39.3 %all-reduce.13.cloned.1.call-done = (f32[180,256]{1,0:T(8,128)}, f32[256,256]{1,0:T(8,128)}) async-done(((f32[180,256]{1,0:T(8,128)}, f32[256,256]{1,0:T(8,128)}), (f32[180,256]{1,0:T(8,128)}, f32[256,256]{1,0:T(8,128)})) %all-reduce.13.cloned.1.call-update) | async-done | bytes 446480 | tf_op jit(solution)/shard_map/psum | solution.py:102
  (171 shorter events, 109.8 us)
Async XLA Ops:
  7.2 133.6 %copy-start = (f32[256,256]{1,0:T(8,128)S(1)}, f32[256,256]{1,0:T(8,128)}, u32[]{:S(2)}) copy-start(f32[256,256]{1,0:T(8,128)} %param.22) | copy-start | bytes 786436
  13.1 37.0 %collective-permute-start = (f32[3,3,60,1,128]{4,3,2,1,0:T(1,128)}, f32[3,3,60,1,128]{4,3,2,1,0:T(1,128)}, u32[]{:S(2)}, u32[]{:S(2)}) collective-permute-start(f32[3,3,60,1,128]{4,3,2,1,0:T(1,128)} %get-tuple-element.51), channel_id=1, source_target_pairs={{0,16},{16,32},{32,48},{48,64},{64,80},{80,96},{96,112},{1,17},{17... | collective-permute-start | bytes 829448 | tf_op jit(solution)/shard_map/ppermute | solution.py:22
  15.5 4.8 copy-start.46
  15.5 34.6 %collective-permute-start.1 = (f32[3,3,60,1,128]{4,3,2,1,0:T(1,128)}, f32[3,3,60,1,128]{4,3,2,1,0:T(1,128)}, u32[]{:S(2)}, u32[]{:S(2)}) collective-permute-start(f32[3,3,60,1,128]{4,3,2,1,0:T(1,128)} %get-tuple-element.52), channel_id=1, source_target_pairs={{16,0},{32,16},{48,32},{64,48},{80,64},{96,80},{112,96},{17,1},{33... | collective-permute-start | bytes 829448 | tf_op jit(solution)/shard_map/ppermute | solution.py:23
  38.1 12.0 %copy-start.40 = (s32[16,128]{1,0:T(8,128)S(1)}, s32[16,128]{1,0:T(8,128)}, u32[]{:S(2)}) copy-start(s32[16,128]{1,0:T(8,128)} %param.15) | copy-start | bytes 24580
  38.1 88.0 %all-to-all-start = ((bf16[128,32,360]{2,1,0:T(8,128)(2,1)}), bf16[128,32,360]{2,1,0:T(8,128)(2,1)S(1)}, u32[]{:S(2)}, u32[]{:S(2)}) async-start(bf16[128,32,360]{2,1,0:T(8,128)(2,1)} %bitcast.94), calls=%async_computation | async-start | bytes 6291456 | tf_op jit(solution)/shard_map/all_to_all | solution.py:84
  50.1 360.5 %all-reduce.15.cloned.1.call-start = ((), (), s32[]{:S(2)}) async-start(), calls=%async_computation.2 | async-start | bytes 901120 | tf_op jit(solution)/shard_map/psum | solution.py:103
  71.1 18.1 %collective-permute-start.2 = (f32[3,3,60,18,1]{2,4,3,1,0:T(1,128)S(1)}, f32[3,3,60,18,1]{2,4,3,1,0:T(1,128)}, u32[]{:S(2)}, u32[]{:S(2)}) collective-permute-start(f32[3,3,60,18,1]{2,4,3,1,0:T(1,128)S(1)} %copy.64), channel_id=1, source_target_pairs={{0,1},{1,2},{2,3},{3,4},{4,5},{5,6},{6,7},{7,8},{8,9},{9,10},{10,1... | collective-permute-start | bytes 116648 | tf_op jit(solution)/shard_map/ppermute | solution.py:22
  79.7 14.7 %collective-permute-start.3 = (f32[3,3,60,18,1]{2,4,3,1,0:T(1,128)}, f32[3,3,60,18,1]{2,4,3,1,0:T(1,128)}, u32[]{:S(2)}, u32[]{:S(2)}) collective-permute-start(f32[3,3,60,18,1]{2,4,3,1,0:T(1,128)} %copy.65), channel_id=1, source_target_pairs={{1,0},{2,1},{3,2},{4,3},{5,4},{6,5},{7,6},{8,7},{9,8},{10,9},{11,1... | collective-permute-start | bytes 116648 | tf_op jit(solution)/shard_map/ppermute | solution.py:23
  138.4 4.3 copy-start.3
  160.4 6.3 %copy-start.16 = (f32[2048,256]{1,0:T(8,128)}, f32[2048,256]{1,0:T(8,128)S(1)}, u32[]{:S(2)}) copy-start(f32[2048,256]{1,0:T(8,128)S(1)} %get-tuple-element.69) | copy-start | bytes 6291460
  174.4 11.8 %copy-start.38 = (f32[16,128]{1,0:T(8,128)S(1)}, f32[16,128]{1,0:T(8,128)}, u32[]{:S(2)}) copy-start(f32[16,128]{1,0:T(8,128)} %param.17) | copy-start | bytes 24580
  174.4 11.8 %copy-start.39 = (f32[16,128]{1,0:T(8,128)S(1)}, f32[16,128]{1,0:T(8,128)}, u32[]{:S(2)}) copy-start(f32[16,128]{1,0:T(8,128)} %param.18) | copy-start | bytes 24580
  191.0 4.9 copy-start.45
  205.4 6.0 %copy-start.7 = (f32[2048,256]{1,0:T(8,128)S(1)}, f32[2048,256]{1,0:T(8,128)}, u32[]{:S(2)}) copy-start(f32[2048,256]{1,0:T(8,128)} %copy-done.6) | copy-start | bytes 6291460
  205.4 6.0 %copy-start.27 = (f32[60,2048]{1,0:T(8,128)S(1)}, f32[60,2048]{1,0:T(8,128)}, u32[]{:S(2)}) copy-start(f32[60,2048]{1,0:T(8,128)} %copy-done.26) | copy-start | bytes 1474564
  213.5 10.5 %copy-start.19 = (f32[2048,256]{1,0:T(8,128)}, f32[2048,256]{1,0:T(8,128)S(1)}, u32[]{:S(2)}) copy-start(f32[2048,256]{1,0:T(8,128)S(1)} %get-tuple-element.71) | copy-start | bytes 6291460
  215.9 4.3 copy-start.18
  321.9 6.5 %copy-start.10 = (f32[1,3,60,16,128]{4,3,2,1,0:T(8,128)S(1)}, f32[1,3,60,16,128]{4,3,2,1,0:T(8,128)}, u32[]{:S(2)}) copy-start(f32[1,3,60,16,128]{4,3,2,1,0:T(8,128)} %get-tuple-element.58) | copy-start | bytes 4423684
  321.9 6.5 %copy-start.15 = (f32[1,3,60,16,128]{4,3,2,1,0:T(8,128)S(1)}, f32[1,3,60,16,128]{4,3,2,1,0:T(8,128)}, u32[]{:S(2)}) copy-start(f32[1,3,60,16,128]{4,3,2,1,0:T(8,128)} %get-tuple-element.33) | copy-start | bytes 4423684
  328.5 4.5 copy-start.30
  328.5 4.5 copy-start.31
  329.7 17.9 %collective-permute-start.4 = (f32[3,3,60,1,128]{4,3,2,1,0:T(1,128)}, f32[3,3,60,1,128]{4,3,2,1,0:T(1,128)}, u32[]{:S(2)}, u32[]{:S(2)}) collective-permute-start(f32[3,3,60,1,128]{4,3,2,1,0:T(1,128)} %get-tuple-element.49), channel_id=1, source_target_pairs={{0,16},{16,32},{32,48},{48,64},{64,80},{80,96},{96,112},{1,17},{17... | collective-permute-start | bytes 829448 | tf_op jit(solution)/shard_map/ppermute | solution.py:22
  331.7 15.9 %collective-permute-start.5 = (f32[3,3,60,1,128]{4,3,2,1,0:T(1,128)}, f32[3,3,60,1,128]{4,3,2,1,0:T(1,128)}, u32[]{:S(2)}, u32[]{:S(2)}) collective-permute-start(f32[3,3,60,1,128]{4,3,2,1,0:T(1,128)} %get-tuple-element.50), channel_id=1, source_target_pairs={{16,0},{32,16},{48,32},{64,48},{80,64},{96,80},{112,96},{17,1},{33... | collective-permute-start | bytes 829448 | tf_op jit(solution)/shard_map/ppermute | solution.py:23
  337.1 3.7 copy-start.35
  340.7 6.2 %copy-start.37 = (f32[256,60]{0,1:T(8,128)S(1)}, f32[256,60]{0,1:T(8,128)}, u32[]{:S(2)}) copy-start(f32[256,60]{0,1:T(8,128)} %get-tuple-element.23) | copy-start | bytes 184324
  340.7 6.9 %copy-start.11 = (f32[1,3,60,16,128]{4,3,2,1,0:T(8,128)S(1)}, f32[1,3,60,16,128]{4,3,2,1,0:T(8,128)}, u32[]{:S(2)}) copy-start(f32[1,3,60,16,128]{4,3,2,1,0:T(8,128)} %get-tuple-element.58) | copy-start | bytes 4423684
  346.9 150.7 %all-reduce.13.cloned.1.call-start = ((), (), s32[]{:S(2)}) async-start(), calls=%async_computation.1 | async-start | bytes 901120 | tf_op jit(solution)/shard_map/psum | solution.py:102
  368.0 42.5 %collective-permute-start.6 = (f32[3,3,60,18,1]{2,4,3,1,0:T(1,128)S(1)}, f32[3,3,60,18,1]{2,4,3,1,0:T(1,128)S(1)}, u32[]{:S(2)}, u32[]{:S(2)}) collective-permute-start(f32[3,3,60,18,1]{2,4,3,1,0:T(1,128)S(1)} %copy.71), channel_id=1, source_target_pairs={{0,1},{1,2},{2,3},{3,4},{4,5},{5,6},{6,7},{7,8},{8,9},{9,10},{10,1... | collective-permute-start | bytes 116648 | tf_op jit(solution)/shard_map/ppermute | solution.py:22
  374.8 40.3 %collective-permute-start.7 = (f32[3,3,60,18,1]{2,4,3,1,0:T(1,128)S(1)}, f32[3,3,60,18,1]{2,4,3,1,0:T(1,128)}, u32[]{:S(2)}, u32[]{:S(2)}) collective-permute-start(f32[3,3,60,18,1]{2,4,3,1,0:T(1,128)S(1)} %copy.72), channel_id=1, source_target_pairs={{1,0},{2,1},{3,2},{4,3},{5,4},{6,5},{7,6},{8,7},{9,8},{10,9},{11,1... | collective-permute-start | bytes 116648 | tf_op jit(solution)/shard_map/ppermute | solution.py:23
  436.5 10.1 %copy-start.22 = (f32[3,60,16,128]{3,2,1,0:T(8,128)S(1)}, f32[3,60,16,128]{3,2,1,0:T(8,128)}, u32[]{:S(2)}) copy-start(f32[3,60,16,128]{3,2,1,0:T(8,128)} %copy-done.21) | copy-start | bytes 4423684
  436.6 10.1 %copy-start.32 = (f32[180,16,128]{2,1,0:T(8,128)S(1)}, f32[180,16,128]{2,1,0:T(8,128)}, u32[]{:S(2)}) copy-start(f32[180,16,128]{2,1,0:T(8,128)} %slice.203) | copy-start | bytes 4423684
  (26 other events, 53.7 us)
Sparse Core Ops, SparseCore 0:
  347.0 63.5 all-reduce.14
  414.3 83.2 all-reduce.12
